TPU v7x, 32 devices: a whole 2x2x4 slice. The times are simulated.
32 devices in a mesh: tm: 8 (over z, x), feat: 4 (over y, core).
Axes of the slice: x: 2, y: 2, z: 4, core: 2. Of those that a mesh axis runs over, the one named last changes fastest.
Arguments:
- coords: float32 [512, 3, 8, 256], P('tm'), may hold values from -12 to 12, as said below
- set_a: int32 [128], replicated, may hold values from 0 to 255
- set_b: int32 [128], replicated, may hold values from 0 to 255
Outputs:
- c00: float32 [16384, 16384], P('feat', 'tm')
- c0t: float32 [16384, 16384], P('feat', 'tm')
Inputs may be any that keep to these rules, and one draw needn't show every extreme that they name: `coords`: positions of a folding protein.
All inputs are finite; a program needn't handle non-finite values.
Results may differ from a plain program's by a relative error of at most 0.0003.
Values may be sent and summed in bfloat16 or wider, within the bound.
A program may use at most 128 MiB of HBM per device.

v0:
```python
import jax
import jax.numpy as jnp
from jax import lax
from jax.sharding import PartitionSpec as P

LAG = 64
contact_radius = 1.2
contact_width = 0.25


def contact_features(positions, index_a, index_b):
    part_a = jnp.take(positions, index_a, axis=3)
    part_b = jnp.take(positions, index_b, axis=3)
    frame_rows = positions.shape[0]
    summed = jnp.zeros((frame_rows, part_a.shape[3], part_b.shape[3]), jnp.float32)
    for first_atom in range(part_a.shape[2]):
        square = jnp.zeros(
            (frame_rows, part_b.shape[2], part_a.shape[3], part_b.shape[3]), jnp.float32
        )
        for component in range(3):
            difference = (
                part_a[:, component, first_atom, :][:, None, :, None]
                - part_b[:, component, :, :][:, :, None, :]
            )
            square = square + difference * difference
        summed = summed + jnp.sum(
            jax.nn.sigmoid((contact_radius - jnp.sqrt(square)) / contact_width), axis=1
        )
    summed = summed / float(part_a.shape[2])
    return summed.reshape(frame_rows, part_a.shape[3] * part_b.shape[3])


def contract_frames(left, right):
    return lax.dot_general(
        left, right, (((0,), (0,)), ((), ())), preferred_element_type=jnp.float32
    )


def pair_sums(frames_block, pairs):
    early = frames_block[:pairs].astype(jnp.float32)
    later = frames_block[LAG:].astype(jnp.float32)
    padding = jnp.zeros((LAG, frames_block.shape[1]), jnp.bfloat16)
    plus = jnp.concatenate([(early + later).astype(jnp.bfloat16), padding], axis=0)
    minus = jnp.concatenate([(early - later).astype(jnp.bfloat16), padding], axis=0)
    return (plus, minus)


def per_device(coords, set_a, set_b):
    feat_count = lax.axis_size("feat")
    feat_index = lax.axis_index("feat")
    rows_a = set_a.shape[0] // feat_count
    index_a = lax.dynamic_slice_in_dim(set_a, feat_index * rows_a, rows_a)
    lifted = contact_features(coords, index_a, set_b)
    frame_rows = coords.shape[0]
    time_count = lax.axis_size("tm")
    time_index = lax.axis_index("tm")
    frames_all = frame_rows * time_count
    pairs = frames_all - LAG
    frame_ids = time_index * frame_rows + jnp.arange(frame_rows, dtype=jnp.int32)
    weight = (frame_ids < pairs).astype(jnp.float32) + (frame_ids >= LAG).astype(jnp.float32)
    local_sums = jnp.dot(weight, lifted, precision=lax.Precision.HIGHEST)
    means = lax.psum(local_sums, "tm") / (2.0 * pairs)
    centered = (lifted - means[None, :]).astype(jnp.bfloat16)
    centered = lax.optimization_barrier(centered)
    every_feature = lax.all_gather(centered, "feat", axis=1, tiled=True)
    column_block = lax.all_to_all(every_feature, "tm", split_axis=1, concat_axis=0, tiled=True)
    plus_cols, minus_cols = pair_sums(column_block, pairs)
    gathered = lax.all_gather(centered, "tm", axis=0, tiled=True)
    plus_rows, minus_rows = pair_sums(gathered, pairs)
    sum_plus = contract_frames(plus_rows, plus_cols)
    sum_minus = contract_frames(minus_rows, minus_cols)
    c00 = (sum_plus + sum_minus) / (4.0 * pairs)
    c0t = (sum_plus - sum_minus) / (4.0 * pairs)
    return (c00, c0t)


def solution(mesh):
    placed = (P("tm", None, None, None), P(), P())
    return jax.shard_map(
        per_device,
        mesh=mesh,
        in_specs=placed,
        out_specs=(P("feat", "tm"), P("feat", "tm")),
        check_vma=False,
    )
```

profile of v0, /device:TPU:0, one launch (start us, length us, event | category | flops | bytes accessed | tf_op | source)
XLA Modules:
  0.0 303.0 jit_solution(4928474648640069345)
XLA Ops:
  7.2 0.7 compare_and_fusion
  7.9 0.7 compare_select_fusion
  8.5 0.7 compare_and_fusion.1
  9.3 2.3 copy.95
  11.6 0.6 gather_fusion
  12.2 0.1 select_bitcast_fusion.1
  12.3 0.3 fusion.34
  12.7 1.9 gather_fusion.1
  14.6 1.6 select_bitcast_fusion
  16.2 0.1 slice_bitcast_fusion.2
  16.3 0.2 copy.98
  17.5 0.1 copy.117
  17.7 0.1 copy.114
  17.9 0.1 copy.112
  18.0 0.1 copy.110
  18.6 0.2 copy.102
  18.8 0.2 copy.100
  19.0 19.8 %fusion.7 = (f32[64,32,128]{2,1,0:T(8,128)S(1)}, f32[64,32,128]{2,1,0:T(8,128)S(1)}, f32[64,32,128]{2,1,0:T(8,128)S(1)}) fusion(f32[64,8,128]{2,1,0:T(8,128)S(1)} %copy.102, f32[64,32]{1,0:T(8,128)S(1)} %copy.101, f32[64,8,128]{2,1,0:T(8,128)S(1)} %copy.100, f32[64,32]{1,0:T(8,128)S(1)} %copy.99, f32[64,8,128]{2,1,0:T(8,128)S(1)} %copy.98, ...), kind=kLoop, calls=%fused_computation.21 | loop fusion | flops 87293952 | bytes 4005888 | tf_op jit(solution)/shard_map/reduce_sum | solution.py:26
  38.8 31.7 %fusion.6 = (f32[64,32,128]{2,1,0:T(8,128)S(1)}, f32[64,32,128]{2,1,0:T(8,128)S(1)}, f32[64,32,128]{2,1,0:T(8,128)S(1)}, f32[64,32,128]{2,1,0:T(8,128)S(1)}, f32[64,32,128]{2,1,0:T(8,128)S(1)}) fusion(f32[64,32]{1,0:T(8,128)S(1)} %copy.105, f32[64,32]{1,0:T(8,128)S(1)} %copy.104, f32[64,32]{1,0:T(8,128)S(1)} %copy.103, f32[64,8,128]{2,1,0:T(8,128)S(1)} %copy.102, ...), kind=kLoop, calls=%fused_computation.19 | loop fusion | flops 145489920 | bytes 6152192 | tf_op jit(solution)/shard_map/reduce_sum | solution.py:26
  70.5 1.0 add_multiply_fusion.1
  71.6 1.2 fusion.18
  72.7 38.8 %psum.7 = f32[4096]{0:T(1024)S(1)} all-reduce(f32[4096]{0:T(1024)S(1)} %bitcast.59), channel_id=1, replica_groups=mesh['tm'=8,'feat'=4] {'tm'}, use_global_device_ids=true, to_apply=%region_8.9 | all-reduce | flops 4096 | bytes 32768 | tf_op jit(solution)/shard_map/psum | solution.py:62
  111.6 1.4 fusion.20
  113.0 0.7 all-gather.3.cloned.1.call-update
  113.7 19.3 %all-gather.5.cloned.1.call-done = bf16[64,16384]{1,0:T(8,128)(2,1)} async-done(((bf16[64,4096]{1,0:T(8,128)(2,1)}), bf16[64,16384]{1,0:T(8,128)(2,1)}) %all-gather.5.cloned.1.call-update) | async-done | bytes 2097168 | tf_op jit(solution)/shard_map/all_gather | solution.py:65
  133.0 1.7 copy.133
  134.7 91.9 %all_to_all.16 = bf16[64,8,2048]{2,0,1:T(8,128)(2,1)S(1)} all-to-all(bf16[64,8,2048]{2,0,1:T(8,128)(2,1)S(1)} %bitcast.55), channel_id=1, replica_groups=mesh['tm'=8,'feat'=4] {'tm'}, dimensions={1} | all-to-all | bytes 4194304 | tf_op jit(solution)/shard_map/all_to_all | solution.py:66
  226.7 2.1 fusion.15
  228.8 11.0 %all-gather.3.cloned.1.call-done = bf16[512,4096]{1,0:T(8,128)(2,1)} async-done(((bf16[64,4096]{1,0:T(8,128)(2,1)}), bf16[512,4096]{1,0:T(8,128)(2,1)}) %all-gather.3.cloned.1.call-update) | async-done | bytes 4194320 | tf_op jit(solution)/shard_map/all_gather | solution.py:68
  239.7 5.5 %fusion.9 = (bf16[448,4096]{1,0:T(8,128)(2,1)S(1)}, bf16[448,4096]{1,0:T(8,128)(2,1)}) fusion(bf16[512,4096]{1,0:T(8,128)(2,1)} %all-gather.3.cloned.1.call-done), kind=kLoop, calls=%fused_computation.23 | loop fusion | flops 11010048 | bytes 14680064 | tf_op jit(solution)/shard_map/convert_element_type | solution.py:44
  245.2 16.3 %fusion.10 = f32[4096,2048]{1,0:T(8,128)} fusion(bf16[448,4096]{1,0:T(8,128)(2,1)S(1)} %get-tuple-element.14, bf16[448,2048]{1,0:T(8,128)(2,1)S(1)} %bitcast.58), kind=kOutput, calls=%fused_computation.26 | convolution fusion | flops 8589934592 | bytes 39059456 | tf_op jit(solution)/shard_map/dot_general | solution.py:34
  261.5 34.7 %subtract_multiply_fusion = (f32[4096,2048]{1,0:T(8,128)}, f32[4096,2048]{1,0:T(8,128)}) fusion(f32[4096,2048]{1,0:T(8,128)} %fusion.10, bf16[448,2048]{1,0:T(8,128)(2,1)S(1)} %bitcast.56, bf16[448,4096]{1,0:T(8,128)(2,1)} %get-tuple-element.15), kind=kOutput, calls=%fused_computation.2 | convolution fusion | flops 8623489024 | bytes 106168320 | tf_op jit(solution)/shard_map/dot_general | solution.py:34
  (29 shorter events, 1.8 us)
Async XLA Ops:
  7.2 125.8 %all-gather.5.cloned.1.call-start = ((), (), s32[]{:S(2)}) async-start(), calls=%async_computation.2 | async-start | bytes 2621440 | tf_op jit(solution)/shard_map/all_gather | solution.py:65
  113.0 126.7 %all-gather.3.cloned.1.call-start = ((), (), s32[]{:S(2)}) async-start(), calls=%async_computation.1 | async-start | bytes 4718592 | tf_op jit(solution)/shard_map/all_gather | solution.py:68
  239.7 5.5 %copy-start = (bf16[7,64,2048]{2,1,0:T(8,128)(2,1)S(1)}, bf16[7,64,2048]{2,1,0:T(8,128)(2,1)}, u32[]{:S(2)}) copy-start(bf16[7,64,2048]{2,1,0:T(8,128)(2,1)} %get-tuple-element.16) | copy-start | bytes 5505028
Sparse Core Ops, SparseCore 0:
  113.1 19.8 all-gather.4
  135.7 103.9 all-gather.2
where the time goes:
time: 303 us
  blocking collectives  131 us (43%)
  other arithmetic  65.3 us (22%)
  matrix products  52.1 us (17%)
  waiting for transfers between devices  30.9 us (10%)
  between operations  14.2 us (5%)
  local copies, waits for them, and re-layouts  9.68 us (3%)
    all_to_all x1, blocking collectives, per_device(): lax.all_to_all(every_feature, 'tm', split_axis=1, concat_axis=0, tiled=True)  91.9 us
    reduce_sum x2, other arithmetic, contact_features(): jnp.sum(jax.nn.sigmoid((contact_radius - jnp.sqrt(square)) / contact_widt...  51.5 us
    dot_general x2, matrix products, contract_frames(): lax.dot_general(left, right, (((0,), (0,)), ((), ())), preferred_element_...  50.9 us
    psum x1, blocking collectives, per_device(): means = lax.psum(local_sums, 'tm') / (2.0 * pairs)  38.8 us
    all_gather x1, waiting for transfers between devices, per_device(): every_feature = lax.all_gather(centered, 'feat', axis=1, tiled=True)  19.3 us
    all_gather x1, waiting for transfers between devices, per_device(): gathered = lax.all_gather(centered, 'tm', axis=0, tiled=True)  11 us
    convert_element_type x2, other arithmetic, pair_sums(): (early - later).astype(jnp.bfloat16)  7.62 us
  transfers between devices with their start and end apart: 2, of which 2 were waited for; matrix products, arithmetic and copies ran while one was open for 1% of the time, Pallas kernels for 0%

commit v1 on v0

--- a/solution.py
+++ b/solution.py
@@ -62,7 +62,8 @@
     means = lax.psum(local_sums, "tm") / (2.0 * pairs)
     centered = (lifted - means[None, :]).astype(jnp.bfloat16)
     centered = lax.optimization_barrier(centered)
-    every_feature = lax.all_gather(centered, "feat", axis=1, tiled=True)
+    parts = lax.all_gather(centered, "feat", axis=0, tiled=False)
+    every_feature = jnp.concatenate(parts, axis=1)
     column_block = lax.all_to_all(every_feature, "tm", split_axis=1, concat_axis=0, tiled=True)
     plus_cols, minus_cols = pair_sums(column_block, pairs)
     gathered = lax.all_gather(centered, "tm", axis=0, tiled=True)

time: 303 us -> 308 us (1.017)
  waiting for transfers between devices: 30.9 us -> 23.8 us
  local copies, waits for them, and re-layouts: 9.68 us -> 15.9 us
  blocking collectives: 131 us -> 136 us
    all_gather x1, waiting for transfers between devices: 11 us -> 3.97 us  [per_device(): gathered = lax.all_gather(centered, 'tm', axis=0, tiled=True)]
    all_to_all x1, blocking collectives: 91.9 us -> 96.9 us  [per_device(): lax.all_to_all(every_feature, 'tm', split_axis=1, concat_axis=0, tiled=True)]
    reshape x0 -> x1, local copies, waits for them, and re-layouts: none -> 3.21 us  [per_device(): every_feature = jnp.concatenate(parts, axis=1)]
  transfers between devices with their start and end apart: 2 -> 2, of which waited for: 2 -> 2; matrix products, arithmetic and copies ran while one was open for 1% -> 3% of each run, Pallas kernels for 0% -> 0%
where the time goes in v1:
time: 308 us; the launch traced here: 307 us
  blocking collectives  136 us (44%)
  other arithmetic  65.3 us (21%)
  matrix products  52.1 us (17%)
  waiting for transfers between devices  23.8 us (8%)
  local copies, waits for them, and re-layouts  15.9 us (5%)
  between operations  14.2 us (5%)
    all_to_all x1, blocking collectives, per_device(): lax.all_to_all(every_feature, 'tm', split_axis=1, concat_axis=0, tiled=True)  96.9 us
    reduce_sum x2, other arithmetic, contact_features(): jnp.sum(jax.nn.sigmoid((contact_radius - jnp.sqrt(square)) / contact_widt...  51.5 us
    dot_general x2, matrix products, contract_frames(): lax.dot_general(left, right, (((0,), (0,)), ((), ())), preferred_element_...  50.9 us
    psum x1, blocking collectives, per_device(): means = lax.psum(local_sums, 'tm') / (2.0 * pairs)  38.8 us
    all_gather x1, waiting for transfers between devices, per_device(): parts = lax.all_gather(centered, 'feat', axis=0, tiled=False)  19.3 us
    convert_element_type x2, other arithmetic, pair_sums(): (early - later).astype(jnp.bfloat16)  7.62 us
  transfers between devices with their start and end apart: 2, of which 2 were waited for; matrix products, arithmetic and copies ran while one was open for 3% of the time, Pallas kernels for 0%

profile of v1, /device:TPU:0, one launch (start us, length us, event | category | flops | bytes accessed | tf_op | source)
XLA Modules:
  0.0 307.2 jit_solution(10904711291934244810)
XLA Ops:
  7.2 0.7 compare_and_fusion
  7.9 0.7 compare_select_fusion
  8.5 0.7 compare_and_fusion.1
  9.3 2.3 copy.99
  11.6 0.6 gather_fusion
  12.2 0.1 select_bitcast_fusion.1
  12.3 0.3 fusion.34
  12.7 1.9 gather_fusion.1
  14.6 1.6 select_bitcast_fusion
  16.2 0.1 slice_bitcast_fusion.2
  16.3 0.2 copy.102
  17.5 0.1 copy.121
  18.6 0.2 copy.106
  18.8 0.2 copy.104
  19.0 19.8 %fusion.7 = (f32[64,32,128]{2,1,0:T(8,128)S(1)}, f32[64,32,128]{2,1,0:T(8,128)S(1)}, f32[64,32,128]{2,1,0:T(8,128)S(1)}) fusion(f32[64,8,128]{2,1,0:T(8,128)S(1)} %copy.106, f32[64,32]{1,0:T(8,128)S(1)} %copy.105, f32[64,8,128]{2,1,0:T(8,128)S(1)} %copy.104, f32[64,32]{1,0:T(8,128)S(1)} %copy.103, f32[64,8,128]{2,1,0:T(8,128)S(1)} %copy.102, ...), kind=kLoop, calls=%fused_computation.21 | loop fusion | flops 87293952 | bytes 4005888 | tf_op jit(solution)/shard_map/reduce_sum | solution.py:26
  38.8 31.7 %fusion.6 = (f32[64,32,128]{2,1,0:T(8,128)S(1)}, f32[64,32,128]{2,1,0:T(8,128)S(1)}, f32[64,32,128]{2,1,0:T(8,128)S(1)}, f32[64,32,128]{2,1,0:T(8,128)S(1)}, f32[64,32,128]{2,1,0:T(8,128)S(1)}) fusion(f32[64,32]{1,0:T(8,128)S(1)} %copy.109, f32[64,32]{1,0:T(8,128)S(1)} %copy.108, f32[64,32]{1,0:T(8,128)S(1)} %copy.107, f32[64,8,128]{2,1,0:T(8,128)S(1)} %copy.106, ...), kind=kLoop, calls=%fused_computation.19 | loop fusion | flops 145489920 | bytes 6152192 | tf_op jit(solution)/shard_map/reduce_sum | solution.py:26
  70.5 1.0 add_multiply_fusion.1
  71.6 1.2 fusion.18
  72.7 38.8 %psum.7 = f32[4096]{0:T(1024)S(1)} all-reduce(f32[4096]{0:T(1024)S(1)} %bitcast.57), channel_id=1, replica_groups=mesh['tm'=8,'feat'=4] {'tm'}, use_global_device_ids=true, to_apply=%region_8.9 | all-reduce | flops 4096 | bytes 32768 | tf_op jit(solution)/shard_map/psum | solution.py:62
  111.6 1.4 fusion.20
  113.0 0.2 all-gather.4.cloned.1.call-start
  113.2 0.5 all-gather.4.cloned.1.call-update
  113.7 19.3 %all-gather.6.cloned.1.call-done = bf16[256,4096]{1,0:T(8,128)(2,1)} async-done(((bf16[64,4096]{1,0:T(8,128)(2,1)}), bf16[256,4096]{1,0:T(8,128)(2,1)}) %all-gather.6.cloned.1.call-update) | async-done | bytes 2097168 | tf_op jit(solution)/shard_map/all_gather | solution.py:65
  133.0 3.2 %copy.128 = bf16[64,4,4096]{2,1,0:T(4,128)(2,1)S(1)} copy(bf16[64,4,4096]{2,0,1:T(8,128)(2,1)} %bitcast.55) | data formatting | bytes 4194304 | tf_op jit(solution)/shard_map/reshape | solution.py:66
  136.2 2.0 all_to_all.12
  138.2 2.7 copy.129
  141.0 96.9 %all_to_all.16 = bf16[64,8,2048]{2,0,1:T(8,128)(2,1)S(1)} all-to-all(bf16[64,8,2048]{2,0,1:T(8,128)(2,1)S(1)} %copy.129), channel_id=1, replica_groups=mesh['tm'=8,'feat'=4] {'tm'}, dimensions={1} | all-to-all | bytes 4194304 | tf_op jit(solution)/shard_map/all_to_all | solution.py:67
  237.8 2.1 fusion.15
  239.9 4.0 %all-gather.4.cloned.1.call-done = bf16[512,4096]{1,0:T(8,128)(2,1)} async-done(((bf16[64,4096]{1,0:T(8,128)(2,1)}), bf16[512,4096]{1,0:T(8,128)(2,1)}) %all-gather.4.cloned.1.call-update) | async-done | bytes 4194320 | tf_op jit(solution)/shard_map/all_gather | solution.py:69
  243.9 5.5 %fusion.9 = (bf16[448,4096]{1,0:T(8,128)(2,1)S(1)}, bf16[448,4096]{1,0:T(8,128)(2,1)}) fusion(bf16[512,4096]{1,0:T(8,128)(2,1)} %all-gather.4.cloned.1.call-done), kind=kLoop, calls=%fused_computation.23 | loop fusion | flops 11010048 | bytes 14680064 | tf_op jit(solution)/shard_map/convert_element_type | solution.py:44
  249.4 16.3 %fusion.10 = f32[4096,2048]{1,0:T(8,128)} fusion(bf16[448,4096]{1,0:T(8,128)(2,1)S(1)} %get-tuple-element.14, bf16[448,2048]{1,0:T(8,128)(2,1)S(1)} %bitcast.56), kind=kOutput, calls=%fused_computation.26 | convolution fusion | flops 8589934592 | bytes 39059456 | tf_op jit(solution)/shard_map/dot_general | solution.py:34
  265.7 34.7 %subtract_multiply_fusion = (f32[4096,2048]{1,0:T(8,128)}, f32[4096,2048]{1,0:T(8,128)}) fusion(f32[4096,2048]{1,0:T(8,128)} %fusion.10, bf16[448,2048]{1,0:T(8,128)(2,1)S(1)} %bitcast.54, bf16[448,4096]{1,0:T(8,128)(2,1)} %get-tuple-element.15), kind=kOutput, calls=%fused_computation.2 | convolution fusion | flops 8623489024 | bytes 106168320 | tf_op jit(solution)/shard_map/dot_general | solution.py:34
  (31 shorter events, 2.0 us)
Async XLA Ops:
  7.2 125.8 %all-gather.6.cloned.1.call-start = ((), (), s32[]{:S(2)}) async-start(), calls=%async_computation.2 | async-start | bytes 2621440 | tf_op jit(solution)/shard_map/all_gather | solution.py:65
  113.0 130.9 %all-gather.4.cloned.1.call-start = ((), (), s32[]{:S(2)}) async-start(), calls=%async_computation.1 | async-start | bytes 4718592 | tf_op jit(solution)/shard_map/all_gather | solution.py:69
  243.9 5.5 %copy-start = (bf16[7,64,2048]{2,1,0:T(8,128)(2,1)S(1)}, bf16[7,64,2048]{2,1,0:T(8,128)(2,1)}, u32[]{:S(2)}) copy-start(bf16[7,64,2048]{2,1,0:T(8,128)(2,1)} %get-tuple-element.16) | copy-start | bytes 5505028
Sparse Core Ops, SparseCore 0:
  113.1 19.8 all-gather.5
  135.7 108.1 all-gather.3
